TPU v7x, 512 devices: a whole 4x4x16 slice. The times are simulated.
512 devices in a mesh: fsdp: 32 (over y, z_hi, x), tensor: 16 (over z_lo, core).
Axes of the slice: x: 4, y: 4, z: 16 (z_hi: 2, z_lo: 8; z = z_hi * 8 + z_lo), core: 2. Of those that a mesh axis runs over, the one named last changes fastest.
Arguments:
- tokens: bfloat16 [512, 9216], P(None, 'tensor'), may hold values from -800 to 800
- ln_gain: bfloat16 [9216], P('tensor'), may hold values from 0.099609375 to 1.8984375
- ln_bias: bfloat16 [9216], P('tensor'), may hold values from -3 to 3
- fc1_weight: bfloat16 [9216, 36864], P('tensor', 'fsdp'), may hold values from -0.0625 to 0.0625
- fc1_bias: bfloat16 [36864], P('fsdp'), may hold values from -3 to 3
- fc2_weight: bfloat16 [36864, 9216], P('fsdp', 'tensor'), may hold values from -0.03125 to 0.03125
- fc2_bias: bfloat16 [9216], P('tensor'), may hold values from -3 to 3
- update_step: float32 [1], replicated, may hold values from -0.004 to 0.004
- perturb_scale: float32 [1], replicated, may hold values from 0.002 to 0.008
- step_seeds: int32 [2], replicated, may hold values from 0 to 16777215
- hash_mults: int32 [3], replicated, may hold values from 65537 to 16777215
Outputs:
- branch_plus: bfloat16 [512, 9216], P('fsdp', 'tensor')
- branch_minus: bfloat16 [512, 9216], P('fsdp', 'tensor')
Inputs may be any that keep to these rules, and one draw needn't show every extreme that they name: `step_seeds`: the previous step's seed, then this step's. `hash_mults`: three multipliers; the lowest bit is set before use.
All inputs are finite; a program needn't handle non-finite values.
Results may differ from a plain program's by a relative error of at most 0.03.
Values may be sent and summed in bfloat16 or wider, within the bound.
No kernel may reach another device: no remote copies, remote signals or barrier semaphores. Data moves between devices by JAX's collectives and lax.ppermute only.
A program may use at most 64 MiB of HBM per device.

v0:
```python
import jax
import jax.numpy as jnp
from jax import lax
from jax.sharding import PartitionSpec as P

D = 9216
FF = 36864


def shift_xor(hashed, amount):
    return hashed ^ lax.shift_right_logical(hashed, jnp.int32(amount))


def hashed_noise(param_index, seed_value, hash_mults):
    mult_a = hash_mults[0] | 1
    mult_b = hash_mults[1] | 1
    mult_c = hash_mults[2] | 1
    hashed = param_index * mult_a + seed_value * mult_b
    hashed = shift_xor(hashed, 16)
    hashed = hashed * mult_c
    hashed = shift_xor(hashed, 13)
    hashed = hashed * mult_a
    hashed = shift_xor(hashed, 16)
    fraction = (hashed & 16777215).astype(jnp.float32) * (1.0 / 16777216.0)
    return (fraction - 0.5) * 3.4641016151377544


def new_weights(weight, param_index, update_step, perturb_scale, step_seeds, hash_mults):
    updated = (
        weight.astype(jnp.float32)
        - update_step[0] * hashed_noise(param_index, step_seeds[0], hash_mults)
    ).astype(jnp.bfloat16)
    updated = lax.optimization_barrier(updated)
    updated_f = updated.astype(jnp.float32)
    shift_term = perturb_scale[0] * hashed_noise(param_index, step_seeds[1], hash_mults)
    return (
        (updated_f + shift_term).astype(jnp.bfloat16),
        (updated_f - shift_term).astype(jnp.bfloat16),
    )


def body(
    tokens,
    ln_gain,
    ln_bias,
    fc1_weight,
    fc1_bias,
    fc2_weight,
    fc2_bias,
    update_step,
    perturb_scale,
    step_seeds,
    hash_mults,
):
    feat_local = tokens.shape[1]
    unit_local = fc1_weight.shape[1]
    values = tokens.astype(jnp.float32)
    totals = lax.psum(jnp.sum(values, axis=1), "tensor")
    row_mean = (totals / D)[:, None]
    centered = values - row_mean
    squares = lax.psum(jnp.sum(centered * centered, axis=1), "tensor")
    row_var = (squares / D)[:, None]
    normed = (
        centered * lax.rsqrt(row_var + 1e-05) * ln_gain.astype(jnp.float32)
        + ln_bias.astype(jnp.float32)
    ).astype(jnp.bfloat16)
    feat_ids = lax.axis_index("tensor") * feat_local + jnp.arange(feat_local, dtype=jnp.int32)
    unit_ids = lax.axis_index("fsdp") * unit_local + jnp.arange(unit_local, dtype=jnp.int32)
    first_index = feat_ids[:, None] * FF + unit_ids[None, :]
    plus_one, minus_one = new_weights(
        fc1_weight, first_index, update_step, perturb_scale, step_seeds, hash_mults
    )
    partial_plus = jnp.dot(normed, plus_one, preferred_element_type=jnp.float32)
    partial_minus = jnp.dot(normed, minus_one, preferred_element_type=jnp.float32)
    bias_one = fc1_bias.astype(jnp.float32)
    sum_plus, sum_minus = (
        lax.psum(partial_plus.astype(jnp.bfloat16), "tensor").astype(jnp.float32),
        lax.psum(partial_minus.astype(jnp.bfloat16), "tensor").astype(jnp.float32),
    )
    hidden_plus = jax.nn.relu(sum_plus + bias_one).astype(jnp.bfloat16)
    hidden_minus = jax.nn.relu(sum_minus + bias_one).astype(jnp.bfloat16)
    second_index = D * FF + unit_ids[:, None] * D + feat_ids[None, :]
    plus_two, minus_two = new_weights(
        fc2_weight, second_index, update_step, perturb_scale, step_seeds, hash_mults
    )
    summed = lax.psum_scatter(
        jnp.concatenate(
            [
                jnp.dot(hidden_plus, plus_two, preferred_element_type=jnp.float32),
                jnp.dot(hidden_minus, minus_two, preferred_element_type=jnp.float32),
            ],
            axis=1,
        ).astype(jnp.bfloat16),
        "fsdp",
        scatter_dimension=0,
        tiled=True,
    ).astype(jnp.float32)
    bias_two = fc2_bias.astype(jnp.float32)
    branch_plus = (summed[:, :feat_local] + bias_two).astype(jnp.bfloat16)
    branch_minus = (summed[:, feat_local:] + bias_two).astype(jnp.bfloat16)
    return (branch_plus, branch_minus)


def solution(mesh):
    in_specs = (
        P(None, "tensor"),
        P("tensor"),
        P("tensor"),
        P("tensor", "fsdp"),
        P("fsdp"),
        P("fsdp", "tensor"),
        P("tensor"),
        P(),
        P(),
        P(),
        P(),
    )
    out_specs = (P("fsdp", "tensor"), P("fsdp", "tensor"))
    return jax.shard_map(body, mesh=mesh, in_specs=in_specs, out_specs=out_specs, check_vma=False)
```

profile of v0, /device:TPU:1, one launch (start us, length us, event | category | flops | bytes accessed | tf_op | source)
XLA Modules:
  0.0 657.9 jit_solution(10783687590641612165)
XLA Ops:
  7.2 0.0 all-reduce.3.cloned.1.call-start
  7.2 1.3 fusion.107
  10.4 1.3 fusion.106
  13.1 3.2 fusion.35
  16.8 0.1 convert_reduce_fusion
  17.0 51.4 %psum.28 = f32[512]{0:T(512)S(1)} all-reduce(f32[512]{0:T(512)S(1)} %convert_reduce_fusion), channel_id=1, replica_groups=mesh['fsdp'=32,'tensor'=16] {'tensor'}, use_global_device_ids=true, to_apply=%region_1.0 | all-reduce | flops 512 | bytes 4096 | tf_op jit(solution)/shard_map/psum | solution.py:58
  68.3 0.2 fusion.72
  68.5 50.4 %psum.29 = f32[512]{0:T(512)S(1)} all-reduce(f32[512]{0:T(512)S(1)} %fusion.72), channel_id=1, replica_groups=mesh['fsdp'=32,'tensor'=16] {'tensor'}, use_global_device_ids=true, to_apply=%region_3.0 | all-reduce | flops 512 | bytes 4096 | tf_op jit(solution)/shard_map/psum | solution.py:61
  119.6 3.4 convolution_convert_fusion
  123.0 3.3 convolution_convert_fusion.1
  126.3 0.0 all-reduce.3.cloned.1.call-update
  126.4 0.2 reduce-scatter.4.cloned.1.call-start
  126.6 1.0 copy-done.1
  127.7 1.8 fusion.34
  129.5 199.1 %all-reduce.3.cloned.1.call-done = (bf16[512,1152]{1,0:T(8,128)(2,1)}, bf16[512,1152]{1,0:T(8,128)(2,1)}) async-done(((bf16[512,1152]{1,0:T(8,128)(2,1)}, bf16[512,1152]{1,0:T(8,128)(2,1)}), (bf16[512,1152]{1,0:T(8,128)(2,1)}, bf16[512,1152]{1,0:T(8,128)(2,1)})) %all-reduce.3.cloned.1.call-update) | async-done | bytes 2359312 | tf_op jit(solution)/shard_map/psum | solution.py:78
  328.6 3.6 fusion.66
  332.2 2.1 fusion.69
  334.3 0.1 pad_maximum_fusion
  334.4 1.4 copy.17
  335.9 312.6 %reduce-scatter.4.cloned.1.call-done = bf16[16,1152]{1,0:T(8,128)(2,1)} async-done(((bf16[512,1152]{1,0:T(8,128)(2,1)}), bf16[16,1152]{1,0:T(8,128)(2,1)}) %reduce-scatter.4.cloned.1.call-update) | async-done | bytes 36880
  648.5 1.0 copy.18
  649.5 0.1 fusion.80
  649.6 0.7 copy.15
  650.4 0.7 copy.16
  (25 shorter events, 0.1 us)
Async XLA Ops:
  7.2 321.4 %all-reduce.3.cloned.1.call-start = ((), (), s32[]{:S(2)}) async-start(), calls=%async_computation.2 | async-start | bytes 4718592 | tf_op jit(solution)/shard_map/psum | solution.py:78
  13.0 3.8 copy-start
  13.1 106.5 %copy-start.3 = (bf16[576]{0:T(1024)(128)(2,1)S(1)}, bf16[576]{0:T(1024)(128)(2,1)}, u32[]{:S(2)}) copy-start(bf16[576]{0:T(1024)(128)(2,1)} %param.12) | copy-start | bytes 3460
  13.1 106.6 %copy-start.4 = (bf16[576]{0:T(1024)(128)(2,1)S(1)}, bf16[576]{0:T(1024)(128)(2,1)}, u32[]{:S(2)}) copy-start(bf16[576]{0:T(1024)(128)(2,1)} %param.13) | copy-start | bytes 3460
  126.3 1.3 copy-start.1
  126.4 522.1 %reduce-scatter.4.cloned.1.call-start = ((), (), s32[]{:S(2)}) async-start(), calls=%async_computation.1 | async-start | bytes 1216512
  127.7 1.8 copy-start.2
  328.6 3.6 copy-start.6
  334.4 1.4 copy-start.5
Sparse Core Ops, SparseCore 0:
  126.5 202.0 all-reduce.2
  336.0 312.4 reduce-scatter.3
where the time goes:
time: 658 us
  waiting for transfers between devices  512 us (78%)
  blocking collectives  102 us (16%)
  between operations  18.6 us (3%)
  matrix products  12.4 us (2%)
  local copies, waits for them, and re-layouts  7.57 us (1%)
    unnamed x3, waiting for transfers between devices  313 us
    psum x1, waiting for transfers between devices, body(): lax.psum(partial_minus.astype(jnp.bfloat16), 'tensor').astype(jnp.float32)  199 us
    psum x1, blocking collectives, body(): totals = lax.psum(jnp.sum(values, axis=1), 'tensor')  51.4 us
    psum x1, blocking collectives, body(): squares = lax.psum(jnp.sum(centered * centered, axis=1), 'tensor')  50.4 us
  transfers between devices with their start and end apart: 2, of which 2 were waited for; matrix products, arithmetic and copies ran while one was open for 0% of the time, Pallas kernels for 0%

commit v1 on v0

--- a/solution.py
+++ b/solution.py
@@ -75,7 +75,9 @@
     bias_one = fc1_bias.astype(jnp.float32)
     sum_plus, sum_minus = (
         lax.psum(partial_plus.astype(jnp.bfloat16), "tensor").astype(jnp.float32),
-        lax.psum(partial_minus.astype(jnp.bfloat16), "tensor").astype(jnp.float32),
+        jnp.sum(lax.all_gather(partial_minus.astype(jnp.bfloat16), "tensor"), axis=0).astype(
+            jnp.float32
+        ),
     )
     hidden_plus = jax.nn.relu(sum_plus + bias_one).astype(jnp.bfloat16)
     hidden_minus = jax.nn.relu(sum_minus + bias_one).astype(jnp.bfloat16)

time: 658 us -> 871 us (1.32)
  waiting for transfers between devices: 512 us -> 712 us
  other arithmetic: 5.64 us -> 19.2 us
    all_gather x0 -> x1, waiting for transfers between devices: none -> 204 us  [body(): lax.all_gather(partial_minus.astype(jnp.bfloat16), 'tensor')]
    reduce_sum x0 -> x1, other arithmetic: none -> 10.1 us  [body(): jnp.sum(lax.all_gather(partial_minus.astype(jnp.bfloat16), 'tensor'), axi...]
    unnamed x3 -> x4, waiting for transfers between devices: 313 us -> 316 us
  transfers between devices with their start and end apart: 2 -> 3, of which waited for: 2 -> 3; matrix products, arithmetic and copies ran while one was open for 0% -> 1% of each run, Pallas kernels for 0% -> 0%
where the time goes in v1:
time: 871 us; the launch traced here: 870 us
  waiting for transfers between devices  712 us (82%)
  blocking collectives  102 us (12%)
  other arithmetic  19.2 us (2%)
  between operations  18.4 us (2%)
  matrix products  12.3 us (1%)
    unnamed x4, waiting for transfers between devices  316 us
    all_gather x1, waiting for transfers between devices, body(): lax.all_gather(partial_minus.astype(jnp.bfloat16), 'tensor')  204 us
    psum x1, waiting for transfers between devices, body(): lax.psum(partial_plus.astype(jnp.bfloat16), 'tensor').astype(jnp.float32)  192 us
    psum x1, blocking collectives, body(): totals = lax.psum(jnp.sum(values, axis=1), 'tensor')  51.4 us
    psum x1, blocking collectives, body(): squares = lax.psum(jnp.sum(centered * centered, axis=1), 'tensor')  50.4 us
  transfers between devices with their start and end apart: 3, of which 3 were waited for; matrix products, arithmetic and copies ran while one was open for 1% of the time, Pallas kernels for 0%

profile of v1, /device:TPU:1, one launch (start us, length us, event | category | flops | bytes accessed | tf_op | source)
XLA Modules:
  0.0 870.5 jit_solution(14308724795223032410)
XLA Ops:
  8.6 1.3 fusion.106
  9.9 1.4 fusion.107
  14.5 1.2 convert_reduce_fusion
  15.7 51.4 %psum.21 = f32[512]{0:T(512)S(1)} all-reduce(f32[512]{0:T(512)S(1)} %convert_reduce_fusion), channel_id=1, replica_groups=mesh['fsdp'=32,'tensor'=16] {'tensor'}, use_global_device_ids=true, to_apply=%region_1.0 | all-reduce | flops 512 | bytes 4096 | tf_op jit(solution)/shard_map/psum | solution.py:58
  67.0 1.3 fusion.72
  68.3 50.4 %psum.22 = f32[512]{0:T(512)S(1)} all-reduce(f32[512]{0:T(512)S(1)} %fusion.72), channel_id=1, replica_groups=mesh['fsdp'=32,'tensor'=16] {'tensor'}, use_global_device_ids=true, to_apply=%region_3.0 | all-reduce | flops 512 | bytes 4096 | tf_op jit(solution)/shard_map/psum | solution.py:61
  118.7 0.7 convert_element_type.91
  119.4 0.7 convert_element_type.92
  120.1 3.1 fusion.35
  123.2 3.3 convolution_convert_fusion.1
  126.7 3.4 convolution_convert_fusion
  130.0 0.2 reduce-scatter.4.cloned.1.call-start
  130.3 1.8 fusion.34
  132.2 191.8 %all-reduce.2.cloned.1.call-done = bf16[512,1152]{1,0:T(8,128)(2,1)} async-done(((bf16[512,1152]{1,0:T(8,128)(2,1)}), bf16[512,1152]{1,0:T(8,128)(2,1)}) %all-reduce.2.cloned.1.call-update) | async-done | bytes 1179664 | tf_op jit(solution)/shard_map/psum | solution.py:77
  324.0 3.5 fusion.66
  327.4 203.7 %all-gather.3.cloned.1.call-done = bf16[8192,1152]{1,0:T(8,128)(2,1)} async-done(((bf16[512,1152]{1,0:T(8,128)(2,1)}), bf16[8192,1152]{1,0:T(8,128)(2,1)}) %all-gather.3.cloned.1.call-update) | async-done | bytes 18874384 | tf_op jit(solution)/shard_map/all_gather | solution.py:78
  531.1 10.1 %reduce_sum.32 = bf16[512,1152]{1,0:T(8,128)(2,1)S(1)} reduce(bf16[16,512,1152]{2,1,0:T(8,128)(2,1)} %bitcast.8, bf16[]{:T(256)} %constant.60.clone.1), dimensions={0}, to_apply=%region_5.0 | reduce | flops 8847360 | bytes 20054018 | tf_op jit(solution)/shard_map/reduce_sum | solution.py:78
  541.2 2.1 fusion.69
  543.5 1.4 copy.17
  544.9 316.4 %reduce-scatter.4.cloned.1.call-done = bf16[16,1152]{1,0:T(8,128)(2,1)} async-done(((bf16[512,1152]{1,0:T(8,128)(2,1)}), bf16[16,1152]{1,0:T(8,128)(2,1)}) %reduce-scatter.4.cloned.1.call-update) | async-done | bytes 36880
  861.3 1.0 copy.18
  862.3 0.1 fusion.80
  862.5 0.7 copy.16
  863.2 0.7 copy.15
  (23 shorter events, 0.3 us)
Async XLA Ops:
  7.2 116.0 %copy-start = (bf16[512,576]{0,1:T(8,128)(2,1)S(1)}, bf16[512,576]{0,1:T(8,128)(2,1)}, u32[]{:S(2)}) copy-start(bf16[512,576]{0,1:T(8,128)(2,1)} %param.11) | copy-start | bytes 1769476
  7.2 316.8 %all-reduce.2.cloned.1.call-start = ((), (), s32[]{:S(2)}) async-start(), calls=%async_computation.1 | async-start | bytes 2359296 | tf_op jit(solution)/shard_map/psum | solution.py:77
  126.6 3.7 copy-start.2
  126.6 3.7 copy-start.1
  126.6 404.5 %all-gather.3.cloned.1.call-start = ((), (), s32[]{:S(2)}) async-start(), calls=%async_computation.2 | async-start | bytes 20054016 | tf_op jit(solution)/shard_map/all_gather | solution.py:78
  130.0 731.3 %reduce-scatter.4.cloned.1.call-start = ((), (), s32[]{:S(2)}) async-start(), calls=%async_computation.3 | async-start | bytes 1216512
  543.4 1.5 copy-start.3
Sparse Core Ops, SparseCore 0:
  126.7 197.2 all-reduce.1
  326.0 205.0 all-gather.2
  545.0 316.2 reduce-scatter.3
